TPU v7x, 256 devices: a whole 4x4x8 slice. The times are simulated.
256 devices in a mesh: energy: 32 (over y, x, core), slab: 8 (over z).
Axes of the slice: x: 4, y: 4, z: 8, core: 2. Of those that a mesh axis runs over, the one named last changes fastest.
Arguments:
- potential_old: float32 [128, 128, 128], P('slab', 'energy'), may hold values from -6 to 6
- charge: float32 [128, 128, 128], P('slab', 'energy'), may hold values from -6 to 6
- permittivity: float32 [128, 128, 128], P('slab', 'energy'), may hold values from 1 to 12
- owner_cell: int32 [32, 256], P('slab'), may hold values from 0 to 65535
- green_free: float32 [32, 32, 2, 256, 256], P('energy', 'slab')
- coupling: float32 [32, 2, 256, 256], P('slab'), may hold values from -0.25 to 0.25
- shifts: int32 [4], replicated, may hold values from 1 to 2, as said below
- occupation: float32 [4], replicated, may hold values from 0.1 to 3
- mode_tiles: float32 [4, 256, 256], replicated, may hold values from -6 to 6
Outputs:
- potential_new: float32 [128, 128, 128], P('slab', 'energy')
- self_energy: float32 [32, 32, 2, 256, 256], P('energy', 'slab')
Inputs may be any that keep to these rules, and one draw needn't show every extreme that they name: `shifts`: every whole number from 1 to 2 is the shift of some mode.
All inputs are finite; a program needn't handle non-finite values.
Results may differ from a plain program's by a relative error of at most 0.00023.
Values sent between devices are 32-bit elements; how exact they have to be, the bound alone decides.
A program may use at most 128 MiB of HBM per device.

v0:
```python
import functools
import math

import jax
import jax.numpy as jnp
from jax import lax
from jax.experimental import pallas as pl
from jax.experimental.pallas import tpu as pltpu
from jax.sharding import PartitionSpec as P

F32 = jnp.float32
BF16 = jnp.bfloat16
MESH = pl.DeviceIdType.MESH
K_PIECES = 4


def split(x):
    high = x.astype(BF16)
    return high, (x - high.astype(F32)).astype(BF16)


def cprod(left, right, transposed=False):
    (ah, al), (bh, bl) = left, right
    n = ah.shape[-1]
    ah, al = ah.reshape(2 * n, n), al.reshape(2 * n, n)
    dims = (((1,), (1 if transposed else 0,)), ((), ()))

    def real(part):
        dot = functools.partial(lax.dot_general, dimension_numbers=dims, preferred_element_type=F32)
        return dot(ah, bh[part]) + dot(al, bh[part]) + dot(ah, bl[part])

    u, w = real(0), real(1)
    return u[:n] - w[n:], u[n:] + w[:n]


def pair_split(parts):
    (rh, rl), (ih, il) = split(parts[0]), split(parts[1])
    return (rh, ih), (rl, il)


def sandwich(link, state):
    inner = cprod(split(state), link, transposed=True)
    return cprod(link, pair_split(inner))


def kernel(
    ne,
    nz,
    pot,
    charge,
    perm,
    owner,
    g_hbm,
    cpl_hbm,
    shifts,
    occ,
    tiles_hbm,
    pot_out,
    se_hbm,
    g,
    cpl,
    tiles,
    hs_lo,
    hs_hi,
    zs_lo,
    zs_hi,
    hr_before,
    hr_after,
    zr_before,
    zr_after,
    pad_f,
    pad_p,
    cells,
    ar_loc,
    ar_mid,
    ar_row,
    ar_col,
    orb,
    g_nb,
    link_h,
    link_l,
    src,
    p_own,
    s_own,
    p_even,
    s_even,
    q_h,
    q_l,
    k_in,
    k_out,
    carry,
    carry_nb,
    greens,
    greens_nb,
    sib_own,
    sib_nb,
    weight,
    se,
    send_sem,
    recv_sem,
    local_sem,
):
    n0, n1, n2 = pot.shape
    slabs, n = owner.shape
    slab_cells = n0 // slabs
    row = min(8, ne)
    cols = ne // row
    e, z = lax.axis_index("energy"), lax.axis_index("slab")
    core = lax.rem(e, 2)
    sibling = (e + 1 - 2 * core, z)
    odd = lax.rem(z, 2) == 1

    def energy(by):
        return (lax.rem(e + (by + ne), ne), z)

    def level(by):
        return (e, lax.rem(z + (by + nz), nz))

    def in_row(k):
        base = (e // row) * row
        return (base + lax.rem(e - base + k, row), z)

    def remote(source, target, index, device):
        return pltpu.make_async_remote_copy(
            src_ref=source,
            dst_ref=target,
            send_sem=send_sem.at[index],
            recv_sem=recv_sem.at[index],
            device_id=device,
            device_id_type=MESH,
        )

    HALO, ROW, COL, GEX = 0, 4, 11, 14
    PAIR = GEX + 2 * slabs
    KUP, KDOWN = PAIR + 2, PAIR + 2 + K_PIECES
    CARRY = KDOWN + K_PIECES
    SIB = CARRY + 2
    SIBN = SIB + slabs

    load_g = pltpu.make_async_copy(g_hbm.at[0], g, local_sem.at[0])
    load_c = pltpu.make_async_copy(cpl_hbm, cpl, local_sem.at[1])
    load_t = pltpu.make_async_copy(tiles_hbm, tiles, local_sem.at[2])
    load_g.start()
    load_c.start()
    load_t.start()

    partners = [in_row(k) for k in range(1, row)] + [energy(row * k) for k in range(1, cols)]
    partners += [energy(by) for by in (1, -1, 2, -2)] + [level(by) for by in (1, -1, 2, -2)]
    barrier = pltpu.get_barrier_semaphore()
    for device in partners:
        pl.semaphore_signal(barrier, inc=1, device_id=device, device_id_type=MESH)

    for index, ref in enumerate((pot, perm)):
        hs_lo[index] = ref[:, 0:1, :]
        hs_hi[index] = ref[:, n1 - 1 : n1, :]
        zs_lo[index] = ref[0]
        zs_hi[index] = ref[n0 - 1]
    pl.semaphore_wait(barrier, len(partners))

    halos = [
        remote(hs_lo, hr_after, HALO, energy(-1)),
        remote(hs_hi, hr_before, HALO + 1, energy(1)),
        remote(zs_lo, zr_after, HALO + 2, level(-1)),
        remote(zs_hi, zr_before, HALO + 3, level(1)),
    ]
    for copy in halos:
        copy.start()

    load_g.wait()
    load_c.wait()

    def make_link(which, s, block):
        made = cprod(split(block), split(cpl[s]))
        for part in range(2):
            link_h[which, s, part], link_l[which, s, part] = split(made[part])

    def make_source(which, s, block):
        scaled = block * orb[pl.ds(s, 1), :]
        made = cprod(split(scaled), split(block))
        for part in range(2):
            src[which, s, part] = block[part] + made[part]

    @pl.loop(0, slabs)
    def _(s):
        make_link(2, s, g[s])

    for copy in halos:
        copy.wait()
    for index, (ref, pad) in enumerate(((pot, pad_f), (perm, pad_p))):
        pad[1 : n0 + 1, 1 : n1 + 1, :] = ref[...]
        pad[1 : n0 + 1, 0:1, :] = jnp.where(e > 0, hr_before[index], 0.0)
        pad[1 : n0 + 1, n1 + 1 : n1 + 2, :] = jnp.where(e < ne - 1, hr_after[index], 0.0)
        pad[0, 1 : n1 + 1, :] = jnp.where(z > 0, zr_before[index], 0.0)
        pad[n0 + 1, 1 : n1 + 1, :] = jnp.where(z < nz - 1, zr_after[index], 0.0)
    centre = perm[...]
    field = pot[...]
    lane = lax.broadcasted_iota(jnp.int32, (n0, n1, n2), 2)
    inner0, inner1 = slice(1, n0 + 1), slice(1, n1 + 1)
    windows = [
        (pad_f[2 : n0 + 2, inner1, :], pad_p[2 : n0 + 2, inner1, :]),
        (pad_f[0:n0, inner1, :], pad_p[0:n0, inner1, :]),
        (pad_f[inner0, 2 : n1 + 2, :], pad_p[inner0, 2 : n1 + 2, :]),
        (pad_f[inner0, 0:n1, :], pad_p[inner0, 0:n1, :]),
    ]
    for shift, edge in ((n2 - 1, n2 - 1), (1, 0)):
        windows.append(
            tuple(jnp.where(lane == edge, 0.0, pltpu.roll(x, shift, 2)) for x in (field, centre))
        )
    numerator = charge[...]
    denominator = jnp.zeros_like(numerator)
    for near_field, near_perm in windows:
        face = 0.5 * (centre + near_perm)
        numerator = numerator + face * near_field
        denominator = denominator + face
    swept = numerator / denominator
    pot_out[...] = swept
    for plane in range(n0):
        cells[pl.ds(plane * n1, n1), :] = swept[plane]

    depth_bits = int(math.log2(n2))
    cross_bits = int(math.log2(n1 * ne))
    rows = slab_cells * n1
    for s in range(slabs):
        index = owner[s : s + 1, :]
        first = index >> (depth_bits + cross_bits)
        second = ((index >> depth_bits) & (n1 * ne - 1)) - e * n1
        third = index & (n2 - 1)
        chosen = jnp.where(
            lax.broadcasted_iota(jnp.int32, (n2, n), 0) == third, 1.0, 0.0
        ).astype(BF16)
        block = cells[pl.ds(s * rows, rows), :]
        high, low = split(block)
        lowest = (block - high.astype(F32) - low.astype(F32)).astype(BF16)
        picked = sum(
            jnp.dot(piece, chosen, preferred_element_type=F32) for piece in (high, low, lowest)
        )
        here = (second >= 0) & (second < n1)
        at = jnp.where(here, first * n1 + second, -1)
        mine = lax.broadcasted_iota(jnp.int32, (rows, n), 0) == at
        ar_loc[s : s + 1, :] = jnp.sum(jnp.where(mine, picked, 0.0), axis=0, keepdims=True)

    row_copies = [remote(ar_loc, ar_row.at[k - 1], ROW + k - 1, in_row(k)) for k in range(1, row)]
    for copy in row_copies:
        copy.start()

    for part in range(2):
        p_own[part] = link_h[2, 0, part].astype(F32) + link_l[2, 0, part].astype(F32)

    @pl.loop(1, slabs)
    def _(s):
        made = cprod((link_h[2, s], link_l[2, s]), split(p_own[...]))
        for part in range(2):
            p_own[part] = made[part]

    send_p = remote(p_own, p_even, PAIR, level(1))

    @pl.when(jnp.logical_not(odd))
    def _():
        send_p.start()

    for copy in row_copies:
        copy.wait()
    total = ar_loc[...]
    for k in range(1, row):
        total = total + ar_row[k - 1]
    ar_mid[...] = total
    col_copies = [
        remote(ar_mid, ar_col.at[k - 1], COL + k - 1, energy(row * k)) for k in range(1, cols)
    ]
    for copy in col_copies:
        copy.start()
    for copy in col_copies:
        copy.wait()
    total = ar_mid[...]
    for k in range(1, cols):
        total = total + ar_col[k - 1]
    orb[...] = total

    def g_copy(s, to_upper):
        side = 0 if to_upper else 1
        return remote(
            g.at[s], g_nb.at[side, s], GEX + side * slabs + s, energy(2 if to_upper else -2)
        )

    for s in range(slabs):
        g_copy(s, True).start()
        g_copy(s, False).start()

    @pl.loop(0, slabs)
    def _(s):
        make_source(2, s, g[s])

    s_own[...] = src[2, 0]

    @pl.loop(1, slabs)
    def _(s):
        made = sandwich((link_h[2, s], link_l[2, s]), s_own[...])
        for part in range(2):
            s_own[part] = made[part] + src[2, s, part]

    send_s = remote(s_own, s_even, PAIR + 1, level(1))

    @pl.when(jnp.logical_not(odd))
    def _():
        send_s.start()

    def make_weights():
        load_t.wait()
        for offset in (1, 2):
            raise_now = jnp.zeros((n, n), F32)
            lower_now = jnp.zeros((n, n), F32)
            for mode in range(tiles.shape[0]):
                hit = jnp.where(shifts[mode] == offset, 1.0, 0.0)
                raise_now = raise_now + (hit * occ[mode]) * tiles[mode]
                lower_now = lower_now + (hit * (occ[mode] + 1.0)) * tiles[mode]
            raise_now = jnp.where(e + offset < ne, raise_now, 0.0)
            lower_now = jnp.where(e >= offset, lower_now, 0.0)
            if offset == 2:
                weight[0], weight[1] = lower_now, raise_now
            else:
                weight[2] = jnp.where(core == 0, raise_now, lower_now)
                weight[3] = jnp.where(core == 0, lower_now, raise_now)

    def prepare_neighbours():
        @pl.loop(0, slabs)
        def _(s):
            for side in range(2):
                g_copy(s, side == 0).wait_recv()
                block = g_nb[side, s]
                make_link(side, s, block)
                make_source(side, s, block)

    early = jnp.logical_or(jnp.logical_not(odd), z == nz - 1)

    make_weights()

    def k_slices():
        half = n // (K_PIECES // 2)
        return [(part, pl.ds(h * half, half)) for part in range(2) for h in range(K_PIECES // 2)]

    def k_up(i):
        at = k_slices()[i]
        return remote(k_out.at[at], k_in.at[at], KUP + i, level(2))

    def k_down(i):
        at = k_slices()[i]
        return remote(k_in.at[at], k_in.at[at], KDOWN + i, level(-1))

    @pl.when(odd)
    def _():
        send_p.wait_recv()
        made = cprod((split(p_own[...])), split(p_even[...]))
        for part in range(2):
            q_h[part], q_l[part] = split(made[part])
        send_s.wait_recv()
        made = sandwich(split(p_own[...]), s_even[...])
        for part in range(2):
            s_own[part] = made[part] + s_own[part]

    @pl.when(early)
    def _():
        prepare_neighbours()

    @pl.when(z == 1)
    def _():
        k_out[...] = s_own[...]
        carry[...] = s_even[...]

    @pl.when(jnp.logical_and(odd, z > 1))
    def _():
        for i in range(K_PIECES):
            k_up(i).wait_recv()
            k_down(i).start()

        @pl.when(z < nz - 1)
        def _():
            made = sandwich((q_h[...], q_l[...]), k_in[...])
            for part in range(2):
                k_out[part] = made[part] + s_own[part]

    @pl.when(jnp.logical_and(odd, z < nz - 1))
    def _():
        for i in range(K_PIECES):
            k_up(i).start()

    @pl.when(jnp.logical_and(odd, z > 1))
    def _():
        made = sandwich(split(p_even[...]), k_in[...])
        for part in range(2):
            carry[part] = made[part] + s_even[part]

    @pl.when(z == 0)
    def _():
        carry[...] = jnp.zeros_like(carry)

    @pl.when(jnp.logical_and(jnp.logical_not(odd), z > 0))
    def _():
        for i in range(K_PIECES):
            k_down(i).wait_recv()
        carry[...] = k_in[...]

    def carry_copy(side):
        return remote(carry, carry_nb.at[side], CARRY + side, energy(2 if side == 0 else -2))

    for side in range(2):
        carry_copy(side).start()

    def own_copy(s):
        return remote(greens.at[s], sib_own.at[s], SIB + s, sibling)

    for s in range(slabs):
        pass

    def own_green(s, before):
        made = sandwich((link_h[2, s], link_l[2, s]), before)
        for part in range(2):
            greens[s, part] = made[part] + src[2, s, part]
        own_copy(s).start()

    own_green(0, carry[...])

    @pl.loop(1, slabs)
    def _(s):
        own_green(s, greens[s - 1])

    @pl.when(jnp.logical_not(early))
    def _():
        prepare_neighbours()

    def carry_arrived(side):
        pltpu.make_async_remote_copy(
            src_ref=carry,
            dst_ref=carry_nb.at[side],
            send_sem=send_sem.at[CARRY + side],
            recv_sem=recv_sem.at[CARRY + side],
            device_id=sibling,
            device_id_type=MESH,
        ).wait_recv()

    def far_copy(side, s):
        return remote(greens_nb.at[side, s], sib_nb.at[s], SIBN + s, sibling)

    def far_green(side, s):
        @pl.when(s == 0)
        def _():
            carry_arrived(side)
            k_in[...] = carry_nb[side]

        made = sandwich((link_h[side, s], link_l[side, s]), k_in[...])
        for part in range(2):
            value = made[part] + src[side, s, part]
            greens_nb[side, s, part] = value
            k_in[part] = value

    @pl.when(jnp.logical_and(odd, z > 1))
    def _():
        for i in range(K_PIECES):
            k_down(i).wait_send()

    @pl.loop(0, slabs)
    def _(s):
        far_green(1 - core, s)
        far_copy(1 - core, s).start()

    def se_copy(s):
        return pltpu.make_async_copy(se.at[s], se_hbm.at[0, s], local_sem.at[3 + s])

    @pl.loop(0, slabs)
    def _(s):
        far_green(core, s)
        own_copy(s).wait_recv()
        far_copy(0, s).wait_recv()
        for part in range(2):
            se[s, part] = (
                weight[0] * greens_nb[0, s, part]
                + weight[1] * greens_nb[1, s, part]
                + weight[2] * sib_own[s, part]
                + weight[3] * sib_nb[s, part]
            )
        se_copy(s).start()

    for s in range(slabs):
        g_copy(s, True).wait_send()
        g_copy(s, False).wait_send()
        own_copy(s).wait_send()
        far_copy(0, s).wait_send()
        se_copy(s).wait()
    for side in range(2):
        carry_copy(side).wait_send()

    @pl.when(jnp.logical_not(odd))
    def _():
        send_p.wait_send()
        send_s.wait_send()

    @pl.when(jnp.logical_and(odd, z < nz - 1))
    def _():
        for i in range(K_PIECES):
            k_up(i).wait_send()


def per_device(
    ne,
    nz,
    potential_old,
    charge,
    permittivity,
    owner_cell,
    green_free,
    coupling,
    shifts,
    occupation,
    mode_tiles,
):
    n0, n1, n2 = potential_old.shape
    slabs, n = owner_cell.shape
    modes = mode_tiles.shape[0]
    vmem = pl.BlockSpec(memory_space=pltpu.VMEM)
    smem = pl.BlockSpec(memory_space=pltpu.SMEM)
    hbm = pl.BlockSpec(memory_space=pl.ANY)
    row = min(8, ne)
    cols = ne // row
    block = (2, n, n)
    sems = 14 + 2 * slabs + 2 + 2 * K_PIECES + 2 + 2 * slabs
    scratch = [
        pltpu.VMEM((slabs,) + block, F32),
        pltpu.VMEM((slabs,) + block, F32),
        pltpu.VMEM((modes, n, n), F32),
        pltpu.VMEM((2, n0, 1, n2), F32),
        pltpu.VMEM((2, n0, 1, n2), F32),
        pltpu.VMEM((2, n1, n2), F32),
        pltpu.VMEM((2, n1, n2), F32),
        pltpu.VMEM((2, n0, 1, n2), F32),
        pltpu.VMEM((2, n0, 1, n2), F32),
        pltpu.VMEM((2, n1, n2), F32),
        pltpu.VMEM((2, n1, n2), F32),
        pltpu.VMEM((n0 + 2, 8, n2), F32),
        pltpu.VMEM((n0 + 2, 8, n2), F32),
        pltpu.VMEM((n0 * n1, n2), F32),
        pltpu.VMEM((slabs, n), F32),
        pltpu.VMEM((slabs, n), F32),
        pltpu.VMEM((row, slabs, n), F32),
        pltpu.VMEM((cols, slabs, n), F32),
        pltpu.VMEM((slabs, n), F32),
        pltpu.VMEM((2, slabs) + block, F32),
        pltpu.VMEM((3, slabs) + block, BF16),
        pltpu.VMEM((3, slabs) + block, BF16),
        pltpu.VMEM((3, slabs) + block, F32),
        pltpu.VMEM(block, F32),
        pltpu.VMEM(block, F32),
        pltpu.VMEM(block, F32),
        pltpu.VMEM(block, F32),
        pltpu.VMEM(block, BF16),
        pltpu.VMEM(block, BF16),
        pltpu.VMEM(block, F32),
        pltpu.VMEM(block, F32),
        pltpu.VMEM(block, F32),
        pltpu.VMEM((2,) + block, F32),
        pltpu.VMEM((slabs,) + block, F32),
        pltpu.VMEM((2, slabs) + block, F32),
        pltpu.VMEM((slabs,) + block, F32),
        pltpu.VMEM((slabs,) + block, F32),
        pltpu.VMEM((4, n, n), F32),
        pltpu.VMEM((slabs,) + block, F32),
        pltpu.SemaphoreType.DMA((sems,)),
        pltpu.SemaphoreType.DMA((sems,)),
        pltpu.SemaphoreType.DMA((3 + slabs,)),
    ]
    return pl.pallas_call(
        functools.partial(kernel, ne, nz),
        out_shape=(
            jax.ShapeDtypeStruct((n0, n1, n2), F32),
            jax.ShapeDtypeStruct((1, slabs) + block, F32),
        ),
        in_specs=[vmem, vmem, vmem, vmem, hbm, hbm, smem, smem, hbm],
        out_specs=(vmem, hbm),
        scratch_shapes=scratch,
        compiler_params=pltpu.CompilerParams(
            collective_id=0, has_side_effects=True, vmem_limit_bytes=60 << 20
        ),
    )(
        potential_old,
        charge,
        permittivity,
        owner_cell,
        green_free,
        coupling,
        shifts,
        occupation,
        mode_tiles,
    )


def solution(mesh):
    in_specs = (
        P("slab", "energy", None),
        P("slab", "energy", None),
        P("slab", "energy", None),
        P("slab", None),
        P("energy", "slab", None, None, None),
        P("slab", None, None, None),
        P(),
        P(),
        P(),
    )
    out_specs = (P("slab", "energy", None), P("energy", "slab", None, None, None))
    return jax.shard_map(
        functools.partial(per_device, mesh.shape["energy"], mesh.shape["slab"]),
        mesh=mesh,
        in_specs=in_specs,
        out_specs=out_specs,
        check_vma=False,
    )
```

profile of v0, /device:TPU:200, one launch (start us, length us, event | category | flops | bytes accessed | tf_op | source)
XLA Modules:
  0.0 115.8 jit_solution(11563361469247919928)
XLA Ops:
  0.6 110.7 %shard_map.104 = (f32[16,4,128]{2,1,0:T(4,128)}, f32[1,4,2,256,256]{4,3,2,1,0:T(8,128)}) custom-call(f32[16,4,128]{2,1,0:T(4,128)} %pot.1, f32[16,4,128]{2,1,0:T(4,128)} %charge.1, f32[16,4,128]{2,1,0:T(4,128)} %perm.1, s32[4,256]{1,0:T(4,128)} %owner.1, f32[1,4,2,256,256]{4,3,2,1,0:T(8,128)} %g_hbm.1, f32[4,2,256,256]{3,2,1,0:T(8,128)} %cpl_hbm.1, ...), custom_call_target="tpu_custom_call" | custom-call | tf_op jit(solution)/shard_map/pallas_call | solution.py:569
  111.3 1.4 %copy.13 = f32[16,4,128]{2,1,0:T(4,128)} copy(f32[16,4,128]{2,1,0:T(4,128)} %get-tuple-element.4) | data formatting | bytes 65536
  112.7 3.0 %copy.14 = f32[1,4,2,256,256]{4,3,2,1,0:T(8,128)} copy(f32[1,4,2,256,256]{4,3,2,1,0:T(8,128)} %get-tuple-element.5) | data formatting | bytes 4194304
where the time goes:
time: 116 us
  Pallas kernels  111 us (96%)
  local copies, waits for them, and re-layouts  4.42 us (4%)
    pallas_call x1, Pallas kernels, per_device(): pl.pallas_call(functools.partial(kernel, ne, nz), out_shape=(jax.ShapeDty...  111 us
    unnamed x2, local copies, waits for them, and re-layouts  4.42 us

commit v1 on v0

--- a/solution.py
+++ b/solution.py
@@ -19,28 +19,17 @@
     return high, (x - high.astype(F32)).astype(BF16)
 
 
+def split3(real, imag):
+    return split(real), split(imag), split(real + imag)
+
+
 def cprod(left, right, transposed=False):
-    (ah, al), (bh, bl) = left, right
-    n = ah.shape[-1]
-    ah, al = ah.reshape(2 * n, n), al.reshape(2 * n, n)
     dims = (((1,), (1 if transposed else 0,)), ((), ()))
-
-    def real(part):
-        dot = functools.partial(lax.dot_general, dimension_numbers=dims, preferred_element_type=F32)
-        return dot(ah, bh[part]) + dot(al, bh[part]) + dot(ah, bl[part])
-
-    u, w = real(0), real(1)
-    return u[:n] - w[n:], u[n:] + w[:n]
-
-
-def pair_split(parts):
-    (rh, rl), (ih, il) = split(parts[0]), split(parts[1])
-    return (rh, ih), (rl, il)
-
-
-def sandwich(link, state):
-    inner = cprod(split(state), link, transposed=True)
-    return cprod(link, pair_split(inner))
+    dot = functools.partial(lax.dot_general, dimension_numbers=dims, preferred_element_type=F32)
+    first, second, third = (
+        dot(a[0], b[0]) + dot(a[1], b[0]) + dot(a[0], b[1]) for a, b in zip(left, right)
+    )
+    return first - second, third - first - second
 
 
 def kernel(
@@ -84,8 +73,9 @@
     s_own,
     p_even,
     s_even,
-    q_h,
-    q_l,
+    map_h,
+    map_l,
+    tmp,
     k_in,
     k_out,
     carry,
@@ -167,22 +157,61 @@
         copy.start()
 
     load_g.wait()
+
+    def g_copy(s, to_upper):
+        side = 0 if to_upper else 1
+        return remote(
+            g.at[s], g_nb.at[side, s], GEX + side * slabs + s, energy(2 if to_upper else -2)
+        )
+
+    for s in range(slabs):
+        g_copy(s, True).start()
+        g_copy(s, False).start()
+
     load_c.wait()
-
-    def make_link(which, s, block):
-        made = cprod(split(block), split(cpl[s]))
-        for part in range(2):
-            link_h[which, s, part], link_l[which, s, part] = split(made[part])
-
-    def make_source(which, s, block):
-        scaled = block * orb[pl.ds(s, 1), :]
-        made = cprod(split(scaled), split(block))
-        for part in range(2):
-            src[which, s, part] = block[part] + made[part]
+    EVEN, ODD, BOTH, HALF = range(4)
+
+    def keep(high, low, at, parts):
+        for k, (h, l) in enumerate(split3(*parts)):
+            high[(*at, k)], low[(*at, k)] = h, l
+
+    def link(which, s):
+        return [(link_h[which, s, k], link_l[which, s, k]) for k in range(3)]
+
+    def mapping(which):
+        return [(map_h[which, k], map_l[which, k]) for k in range(3)]
+
+    def three(ref, *at):
+        return split3(ref[(*at, 0)], ref[(*at, 1)])
+
+    def sandwiches(*jobs):
+        for slot, (outer, state, _) in enumerate(jobs):
+            tmp[slot, 0], tmp[slot, 1] = cprod(state(), outer(), transposed=True)
+        for slot, (outer, _, write) in enumerate(jobs):
+            write(*cprod(outer(), three(tmp, slot)))
+
+    def added(target, at, *terms):
+        def write(real, imag):
+            for part, value in enumerate((real, imag)):
+                target[(*at, part)] = value + sum(ref[(*where, part)] for ref, where in terms)
+
+        return write
+
+    def make_links(s, *pairs):
+        factor = three(cpl, s)
+        for which, ref, at in pairs:
+            keep(link_h, link_l, (which, s), cprod(three(ref, *at), factor))
+
+    def make_sources(s, *pairs):
+        scale = orb[pl.ds(s, 1), :]
+        for which, ref, at in pairs:
+            real, imag = ref[(*at, 0)], ref[(*at, 1)]
+            made = cprod(split3(real * scale, imag * scale), split3(real, imag))
+            src[which, s, 0], src[which, s, 1] = real + made[0], imag + made[1]
 
     @pl.loop(0, slabs)
     def _(s):
-        make_link(2, s, g[s])
+        make_links(s, (2, g, (s,)))
 
     for copy in halos:
         copy.wait()
@@ -243,14 +272,9 @@
     for copy in row_copies:
         copy.start()
 
-    for part in range(2):
-        p_own[part] = link_h[2, 0, part].astype(F32) + link_l[2, 0, part].astype(F32)
-
-    @pl.loop(1, slabs)
-    def _(s):
-        made = cprod((link_h[2, s], link_l[2, s]), split(p_own[...]))
-        for part in range(2):
-            p_own[part] = made[part]
+    tmp[0, 0], tmp[0, 1] = cprod(link(2, 1), link(2, 0))
+    keep(map_h, map_l, (HALF,), cprod(link(2, 3), link(2, 2)))
+    p_own[0], p_own[1] = cprod(mapping(HALF), three(tmp, 0))
 
     send_p = remote(p_own, p_even, PAIR, level(1))
 
@@ -276,27 +300,15 @@
         total = total + ar_col[k - 1]
     orb[...] = total
 
-    def g_copy(s, to_upper):
-        side = 0 if to_upper else 1
-        return remote(
-            g.at[s], g_nb.at[side, s], GEX + side * slabs + s, energy(2 if to_upper else -2)
-        )
-
-    for s in range(slabs):
-        g_copy(s, True).start()
-        g_copy(s, False).start()
-
     @pl.loop(0, slabs)
     def _(s):
-        make_source(2, s, g[s])
-
-    s_own[...] = src[2, 0]
-
-    @pl.loop(1, slabs)
-    def _(s):
-        made = sandwich((link_h[2, s], link_l[2, s]), s_own[...])
-        for part in range(2):
-            s_own[part] = made[part] + src[2, s, part]
+        make_sources(s, (2, g, (s,)))
+
+    sandwiches(
+        (lambda: link(2, 1), lambda: three(src, 2, 0), added(carry, (), (src, (2, 1)))),
+        (lambda: link(2, 3), lambda: three(src, 2, 2), added(k_out, (), (src, (2, 3)))),
+    )
+    sandwiches((lambda: mapping(HALF), lambda: three(carry), added(s_own, (), (k_out, ()))))
 
     send_s = remote(s_own, s_even, PAIR + 1, level(1))
 
@@ -326,9 +338,9 @@
         def _(s):
             for side in range(2):
                 g_copy(s, side == 0).wait_recv()
-                block = g_nb[side, s]
-                make_link(side, s, block)
-                make_source(side, s, block)
+            both = [(side, g_nb, (side, s)) for side in range(2)]
+            make_links(s, *both)
+            make_sources(s, *both)
 
     early = jnp.logical_or(jnp.logical_not(odd), z == nz - 1)
 
@@ -349,13 +361,11 @@
     @pl.when(odd)
     def _():
         send_p.wait_recv()
-        made = cprod((split(p_own[...])), split(p_even[...]))
-        for part in range(2):
-            q_h[part], q_l[part] = split(made[part])
+        keep(map_h, map_l, (ODD,), (p_own[0], p_own[1]))
+        keep(map_h, map_l, (EVEN,), (p_even[0], p_even[1]))
+        keep(map_h, map_l, (BOTH,), cprod(mapping(ODD), mapping(EVEN)))
         send_s.wait_recv()
-        made = sandwich(split(p_own[...]), s_even[...])
-        for part in range(2):
-            s_own[part] = made[part] + s_own[part]
+        sandwiches((lambda: mapping(ODD), lambda: three(s_even), added(s_own, (), (s_own, ()))))
 
     @pl.when(early)
     def _():
@@ -374,9 +384,7 @@
 
         @pl.when(z < nz - 1)
         def _():
-            made = sandwich((q_h[...], q_l[...]), k_in[...])
-            for part in range(2):
-                k_out[part] = made[part] + s_own[part]
+            sandwiches((lambda: mapping(BOTH), lambda: three(k_in), added(k_out, (), (s_own, ()))))
 
     @pl.when(jnp.logical_and(odd, z < nz - 1))
     def _():
@@ -385,9 +393,7 @@
 
     @pl.when(jnp.logical_and(odd, z > 1))
     def _():
-        made = sandwich(split(p_even[...]), k_in[...])
-        for part in range(2):
-            carry[part] = made[part] + s_even[part]
+        sandwiches((lambda: mapping(EVEN), lambda: three(k_in), added(carry, (), (s_even, ()))))
 
     @pl.when(z == 0)
     def _():
@@ -408,20 +414,17 @@
     def own_copy(s):
         return remote(greens.at[s], sib_own.at[s], SIB + s, sibling)
 
-    for s in range(slabs):
-        pass
-
-    def own_green(s, before):
-        made = sandwich((link_h[2, s], link_l[2, s]), before)
-        for part in range(2):
-            greens[s, part] = made[part] + src[2, s, part]
+    def own_green(s, ref, at):
+        sandwiches(
+            (lambda: link(2, s), lambda: three(ref, *at), added(greens, (s,), (src, (2, s))))
+        )
         own_copy(s).start()
 
-    own_green(0, carry[...])
+    own_green(0, carry, ())
 
     @pl.loop(1, slabs)
     def _(s):
-        own_green(s, greens[s - 1])
+        own_green(s, greens, (s - 1,))
 
     @pl.when(jnp.logical_not(early))
     def _():
@@ -440,34 +443,23 @@
     def far_copy(side, s):
         return remote(greens_nb.at[side, s], sib_nb.at[s], SIBN + s, sibling)
 
-    def far_green(side, s):
-        @pl.when(s == 0)
-        def _():
-            carry_arrived(side)
-            k_in[...] = carry_nb[side]
-
-        made = sandwich((link_h[side, s], link_l[side, s]), k_in[...])
-        for part in range(2):
-            value = made[part] + src[side, s, part]
-            greens_nb[side, s, part] = value
-            k_in[part] = value
-
-    @pl.when(jnp.logical_and(odd, z > 1))
-    def _():
-        for i in range(K_PIECES):
-            k_down(i).wait_send()
-
-    @pl.loop(0, slabs)
-    def _(s):
-        far_green(1 - core, s)
+    def far_greens(s, ref, at):
+        sandwiches(
+            *(
+                (
+                    lambda side=side: link(side, s),
+                    lambda side=side: three(ref, side, *at),
+                    added(greens_nb, (side, s), (src, (side, s))),
+                )
+                for side in range(2)
+            )
+        )
         far_copy(1 - core, s).start()
 
     def se_copy(s):
         return pltpu.make_async_copy(se.at[s], se_hbm.at[0, s], local_sem.at[3 + s])
 
-    @pl.loop(0, slabs)
-    def _(s):
-        far_green(core, s)
+    def mix(s):
         own_copy(s).wait_recv()
         far_copy(0, s).wait_recv()
         for part in range(2):
@@ -479,6 +471,17 @@
             )
         se_copy(s).start()
 
+    for side in range(2):
+        carry_arrived(side)
+    far_greens(0, carry_nb, ())
+
+    @pl.loop(1, slabs)
+    def _(s):
+        far_greens(s, greens_nb, (s - 1,))
+        mix(s - 1)
+
+    mix(slabs - 1)
+
     for s in range(slabs):
         g_copy(s, True).wait_send()
         g_copy(s, False).wait_send()
@@ -497,6 +500,11 @@
     def _():
         for i in range(K_PIECES):
             k_up(i).wait_send()
+
+    @pl.when(jnp.logical_and(odd, z > 1))
+    def _():
+        for i in range(K_PIECES):
+            k_down(i).wait_send()
 
 
 def per_device(
@@ -543,15 +551,16 @@
         pltpu.VMEM((cols, slabs, n), F32),
         pltpu.VMEM((slabs, n), F32),
         pltpu.VMEM((2, slabs) + block, F32),
-        pltpu.VMEM((3, slabs) + block, BF16),
-        pltpu.VMEM((3, slabs) + block, BF16),
+        pltpu.VMEM((3, slabs, 3, n, n), BF16),
+        pltpu.VMEM((3, slabs, 3, n, n), BF16),
         pltpu.VMEM((3, slabs) + block, F32),
         pltpu.VMEM(block, F32),
         pltpu.VMEM(block, F32),
         pltpu.VMEM(block, F32),
         pltpu.VMEM(block, F32),
-        pltpu.VMEM(block, BF16),
-        pltpu.VMEM(block, BF16),
+        pltpu.VMEM((4, 3, n, n), BF16),
+        pltpu.VMEM((4, 3, n, n), BF16),
+        pltpu.VMEM((2,) + block, F32),
         pltpu.VMEM(block, F32),
         pltpu.VMEM(block, F32),
         pltpu.VMEM(block, F32),

time: 116 us -> 143 us (1.23)
  the two profiles are of different devices: /device:TPU:200 before, /device:TPU:193 now
where the time goes in v1:
time: 143 us
  Pallas kernels  138 us (97%)
  local copies, waits for them, and re-layouts  4.42 us (3%)
    pallas_call x1, Pallas kernels, per_device(): pl.pallas_call(functools.partial(kernel, ne, nz), out_shape=(jax.ShapeDty...  138 us
    unnamed x2, local copies, waits for them, and re-layouts  4.42 us

profile of v1, /device:TPU:193, one launch (start us, length us, event | category | flops | bytes accessed | tf_op | source)
XLA Modules:
  0.0 142.7 jit_solution(17927127601000838347)
XLA Ops:
  0.6 137.6 %shard_map.104 = (f32[16,4,128]{2,1,0:T(4,128)}, f32[1,4,2,256,256]{4,3,2,1,0:T(8,128)}) custom-call(f32[16,4,128]{2,1,0:T(4,128)} %pot.1, f32[16,4,128]{2,1,0:T(4,128)} %charge.1, f32[16,4,128]{2,1,0:T(4,128)} %perm.1, s32[4,256]{1,0:T(4,128)} %owner.1, f32[1,4,2,256,256]{4,3,2,1,0:T(8,128)} %g_hbm.1, f32[4,2,256,256]{3,2,1,0:T(8,128)} %cpl_hbm.1, ...), custom_call_target="tpu_custom_call" | custom-call | tf_op jit(solution)/shard_map/pallas_call | solution.py:578
  138.3 1.4 copy.13
  139.6 3.0 %copy.14 = f32[1,4,2,256,256]{4,3,2,1,0:T(8,128)} copy(f32[1,4,2,256,256]{4,3,2,1,0:T(8,128)} %get-tuple-element.5) | data formatting | bytes 4194304

commit v2 on v1

--- a/solution.py
+++ b/solution.py
@@ -11,7 +11,7 @@
 F32 = jnp.float32
 BF16 = jnp.bfloat16
 MESH = pl.DeviceIdType.MESH
-K_PIECES = 4
+K_PIECES = 8
 
 
 def split(x):
@@ -76,10 +76,11 @@
     map_h,
     map_l,
     tmp,
+    map_in,
+    state_in,
     k_in,
     k_out,
     carry,
-    carry_nb,
     greens,
     greens_nb,
     sib_own,
@@ -93,6 +94,7 @@
     n0, n1, n2 = pot.shape
     slabs, n = owner.shape
     slab_cells = n0 // slabs
+    assert (nz, slabs) == (8, 4)
     row = min(8, ne)
     cols = ne // row
     e, z = lax.axis_index("energy"), lax.axis_index("slab")
@@ -122,8 +124,10 @@
 
     HALO, ROW, COL, GEX = 0, 4, 11, 14
     PAIR = GEX + 2 * slabs
-    KUP, KDOWN = PAIR + 2, PAIR + 2 + K_PIECES
-    CARRY = KDOWN + K_PIECES
+    KUP, KDOWN, KBACK = (PAIR + 2 + i * K_PIECES for i in range(3))
+    KSIDE = KUP
+    AHEAD = KBACK + K_PIECES
+    CARRY = AHEAD + 2
     SIB = CARRY + 2
     SIBN = SIB + slabs
 
@@ -163,10 +167,6 @@
         return remote(
             g.at[s], g_nb.at[side, s], GEX + side * slabs + s, energy(2 if to_upper else -2)
         )
-
-    for s in range(slabs):
-        g_copy(s, True).start()
-        g_copy(s, False).start()
 
     load_c.wait()
     EVEN, ODD, BOTH, HALF = range(4)
@@ -278,7 +278,7 @@
 
     send_p = remote(p_own, p_even, PAIR, level(1))
 
-    @pl.when(jnp.logical_not(odd))
+    @pl.when(jnp.logical_and(jnp.logical_not(odd), z > 0))
     def _():
         send_p.start()
 
@@ -300,6 +300,10 @@
         total = total + ar_col[k - 1]
     orb[...] = total
 
+    for s in range(1, slabs):
+        g_copy(s, True).start()
+        g_copy(s, False).start()
+
     @pl.loop(0, slabs)
     def _(s):
         make_sources(s, (2, g, (s,)))
@@ -334,7 +338,7 @@
                 weight[3] = jnp.where(core == 0, lower_now, raise_now)
 
     def prepare_neighbours():
-        @pl.loop(0, slabs)
+        @pl.loop(1, slabs)
         def _(s):
             for side in range(2):
                 g_copy(s, side == 0).wait_recv()
@@ -342,74 +346,148 @@
             make_links(s, *both)
             make_sources(s, *both)
 
-    early = jnp.logical_or(jnp.logical_not(odd), z == nz - 1)
-
     make_weights()
 
     def k_slices():
-        half = n // (K_PIECES // 2)
-        return [(part, pl.ds(h * half, half)) for part in range(2) for h in range(K_PIECES // 2)]
-
-    def k_up(i):
+        rows_each = n // (K_PIECES // 2)
+        return [
+            (part, pl.ds(h * rows_each, rows_each))
+            for h in range(K_PIECES // 2)
+            for part in range(2)
+        ]
+
+    def k_piece(source, first, i, device):
         at = k_slices()[i]
-        return remote(k_out.at[at], k_in.at[at], KUP + i, level(2))
-
-    def k_down(i):
-        at = k_slices()[i]
-        return remote(k_in.at[at], k_in.at[at], KDOWN + i, level(-1))
-
-    @pl.when(odd)
-    def _():
-        send_p.wait_recv()
+        return remote(source.at[at], k_in.at[at], first + i, device)
+
+    pieces = range(K_PIECES)
+    k_up = [k_piece(k_out, KUP, i, level(2)) for i in pieces]
+    k_down = [k_piece(k_in, KDOWN, i, level(-1)) for i in pieces]
+    k_side = [k_piece(k_in, KSIDE, i, level(1)) for i in pieces]
+    k_back = [k_piece(k_out, KBACK, i, level(-2)) for i in pieces]
+    k_relay = [k_piece(k_in, KBACK, i, level(-2)) for i in pieces]
+    ahead = [
+        remote(p_even, map_in, AHEAD, level(1)),
+        remote(s_own, state_in, AHEAD + 1, level(1)),
+    ]
+    ahead_relay = [
+        remote(map_in, map_in, AHEAD, level(1)),
+        remote(state_in, state_in, AHEAD + 1, level(1)),
+    ]
+
+    def pair_state():
         keep(map_h, map_l, (ODD,), (p_own[0], p_own[1]))
-        keep(map_h, map_l, (EVEN,), (p_even[0], p_even[1]))
-        keep(map_h, map_l, (BOTH,), cprod(mapping(ODD), mapping(EVEN)))
         send_s.wait_recv()
         sandwiches((lambda: mapping(ODD), lambda: three(s_even), added(s_own, (), (s_own, ()))))
 
+    def pair_maps():
+        send_p.wait_recv()
+        keep(map_h, map_l, (EVEN,), (p_even[0], p_even[1]))
+
+    def into_carry(which, state):
+        sandwiches((lambda: mapping(which), lambda: three(k_in), added(carry, (), (state, ()))))
+
+    def receive_and_hand_on(copies, *onward):
+        for i in pieces:
+            copies[i].wait_recv()
+            for copy in onward:
+                copy[i].start()
+
+    early = jnp.logical_or(jnp.logical_not(odd), z > 4)
+
+    @pl.when(z == 0)
+    def _():
+        carry[...] = jnp.zeros_like(carry)
+
+    @pl.when(z == 1)
+    def _():
+        pair_state()
+        k_out[...] = s_own[...]
+        for copy in k_up:
+            copy.start()
+        carry[...] = s_even[...]
+
+    @pl.when(jnp.logical_or(z == 3, z == 5))
+    def _():
+        pair_maps()
+        keep(map_h, map_l, (ODD,), (p_own[0], p_own[1]))
+        both = cprod(mapping(ODD), mapping(EVEN))
+
+        @pl.when(z == 3)
+        def _():
+            keep(map_h, map_l, (BOTH,), both)
+
+        @pl.when(z == 5)
+        def _():
+            p_even[0], p_even[1] = both
+            ahead[0].start()
+
+        pair_state()
+
+        @pl.when(z == 5)
+        def _():
+            ahead[1].start()
+
+    @pl.when(z == 7)
+    def _():
+        pair_maps()
+        send_s.wait_recv()
+        ahead[0].wait_recv()
+        keep(map_h, map_l, (BOTH,), cprod(mapping(EVEN), three(map_in)))
+
+    @pl.when(z == 6)
+    def _():
+        for copy, relay in zip(ahead, ahead_relay):
+            copy.wait_recv()
+            relay.start()
+        keep(map_h, map_l, (BOTH,), (map_in[0], map_in[1]))
+
     @pl.when(early)
     def _():
         prepare_neighbours()
 
-    @pl.when(z == 1)
-    def _():
-        k_out[...] = s_own[...]
-        carry[...] = s_even[...]
-
-    @pl.when(jnp.logical_and(odd, z > 1))
-    def _():
-        for i in range(K_PIECES):
-            k_up(i).wait_recv()
-            k_down(i).start()
-
-        @pl.when(z < nz - 1)
-        def _():
-            sandwiches((lambda: mapping(BOTH), lambda: three(k_in), added(k_out, (), (s_own, ()))))
-
-    @pl.when(jnp.logical_and(odd, z < nz - 1))
-    def _():
-        for i in range(K_PIECES):
-            k_up(i).start()
-
-    @pl.when(jnp.logical_and(odd, z > 1))
-    def _():
-        sandwiches((lambda: mapping(EVEN), lambda: three(k_in), added(carry, (), (s_even, ()))))
-
-    @pl.when(z == 0)
-    def _():
-        carry[...] = jnp.zeros_like(carry)
-
-    @pl.when(jnp.logical_and(jnp.logical_not(odd), z > 0))
-    def _():
-        for i in range(K_PIECES):
-            k_down(i).wait_recv()
+    @pl.when(z == 3)
+    def _():
+        receive_and_hand_on(k_up, k_down)
+        sandwiches((lambda: mapping(BOTH), lambda: three(k_in), added(k_out, (), (s_own, ()))))
+        for forward, backward in zip(k_up, k_back):
+            backward.start()
+            forward.start()
+
+    @pl.when(z == 5)
+    def _():
+        receive_and_hand_on(k_up, k_side, k_down)
+
+    @pl.when(jnp.logical_or(z == 3, z == 5))
+    def _():
+        into_carry(EVEN, s_even)
+
+    @pl.when(z == 7)
+    def _():
+        ahead[1].wait_recv()
+        sandwiches(
+            (lambda: mapping(EVEN), lambda: three(state_in), added(k_out, (), (s_even, ())))
+        )
+        receive_and_hand_on(k_back)
+        into_carry(BOTH, k_out)
+
+    @pl.when(jnp.logical_or(z == 2, z == 4))
+    def _():
+        receive_and_hand_on(k_down)
         carry[...] = k_in[...]
 
-    def carry_copy(side):
-        return remote(carry, carry_nb.at[side], CARRY + side, energy(2 if side == 0 else -2))
-
-    for side in range(2):
-        carry_copy(side).start()
+    @pl.when(z == 6)
+    def _():
+        receive_and_hand_on(k_side)
+        into_carry(BOTH, state_in)
+
+    def first_copy(side):
+        return remote(
+            greens.at[0],
+            greens_nb.at[side, 0],
+            CARRY + side,
+            energy(2 if side == 0 else -2),
+        )
 
     def own_copy(s):
         return remote(greens.at[s], sib_own.at[s], SIB + s, sibling)
@@ -418,43 +496,36 @@
         sandwiches(
             (lambda: link(2, s), lambda: three(ref, *at), added(greens, (s,), (src, (2, s))))
         )
-        own_copy(s).start()
 
     own_green(0, carry, ())
+    for side in range(2):
+        first_copy(side).start()
+    own_copy(0).start()
 
     @pl.loop(1, slabs)
     def _(s):
         own_green(s, greens, (s - 1,))
+        own_copy(s).start()
+
+    @pl.when(z == 1)
+    def _():
+        receive_and_hand_on(k_back, k_relay)
 
     @pl.when(jnp.logical_not(early))
     def _():
         prepare_neighbours()
-
-    def carry_arrived(side):
-        pltpu.make_async_remote_copy(
-            src_ref=carry,
-            dst_ref=carry_nb.at[side],
-            send_sem=send_sem.at[CARRY + side],
-            recv_sem=recv_sem.at[CARRY + side],
-            device_id=sibling,
-            device_id_type=MESH,
-        ).wait_recv()
 
     def far_copy(side, s):
         return remote(greens_nb.at[side, s], sib_nb.at[s], SIBN + s, sibling)
 
-    def far_greens(s, ref, at):
+    def far_green(side, s):
         sandwiches(
-            *(
-                (
-                    lambda side=side: link(side, s),
-                    lambda side=side: three(ref, side, *at),
-                    added(greens_nb, (side, s), (src, (side, s))),
-                )
-                for side in range(2)
+            (
+                lambda: link(side, s),
+                lambda: three(greens_nb, side, s - 1),
+                added(greens_nb, (side, s), (src, (side, s))),
             )
         )
-        far_copy(1 - core, s).start()
 
     def se_copy(s):
         return pltpu.make_async_copy(se.at[s], se_hbm.at[0, s], local_sem.at[3 + s])
@@ -472,39 +543,46 @@
         se_copy(s).start()
 
     for side in range(2):
-        carry_arrived(side)
-    far_greens(0, carry_nb, ())
+        first_copy(side).wait_recv()
+    far_copy(1 - core, 0).start()
 
     @pl.loop(1, slabs)
     def _(s):
-        far_greens(s, greens_nb, (s - 1,))
+        far_green(1 - core, s)
+        far_copy(1 - core, s).start()
+
+    @pl.loop(1, slabs)
+    def _(s):
+        far_green(core, s)
         mix(s - 1)
 
     mix(slabs - 1)
 
     for s in range(slabs):
-        g_copy(s, True).wait_send()
-        g_copy(s, False).wait_send()
         own_copy(s).wait_send()
         far_copy(0, s).wait_send()
         se_copy(s).wait()
+    for s in range(1, slabs):
+        g_copy(s, True).wait_send()
+        g_copy(s, False).wait_send()
     for side in range(2):
-        carry_copy(side).wait_send()
-
-    @pl.when(jnp.logical_not(odd))
-    def _():
-        send_p.wait_send()
-        send_s.wait_send()
-
-    @pl.when(jnp.logical_and(odd, z < nz - 1))
-    def _():
-        for i in range(K_PIECES):
-            k_up(i).wait_send()
-
-    @pl.when(jnp.logical_and(odd, z > 1))
-    def _():
-        for i in range(K_PIECES):
-            k_down(i).wait_send()
+        first_copy(side).wait_send()
+
+    def sent(condition, *copies):
+        @pl.when(condition)
+        def _():
+            for copy in copies:
+                copy.wait_send()
+
+    sent(jnp.logical_not(odd), send_s)
+    sent(jnp.logical_and(jnp.logical_not(odd), z > 0), send_p)
+    sent(jnp.logical_or(z == 1, z == 3), *k_up)
+    sent(jnp.logical_or(z == 3, z == 5), *k_down)
+    sent(z == 5, *k_side)
+    sent(z == 3, *k_back)
+    sent(z == 1, *k_relay)
+    sent(z == 5, *ahead)
+    sent(z == 6, *ahead_relay)
 
 
 def per_device(
@@ -529,7 +607,7 @@
     row = min(8, ne)
     cols = ne // row
     block = (2, n, n)
-    sems = 14 + 2 * slabs + 2 + 2 * K_PIECES + 2 + 2 * slabs
+    sems = 14 + 2 * slabs + 2 + 3 * K_PIECES + 2 + 2 + 2 * slabs
     scratch = [
         pltpu.VMEM((slabs,) + block, F32),
         pltpu.VMEM((slabs,) + block, F32),
@@ -564,7 +642,8 @@
         pltpu.VMEM(block, F32),
         pltpu.VMEM(block, F32),
         pltpu.VMEM(block, F32),
-        pltpu.VMEM((2,) + block, F32),
+        pltpu.VMEM(block, F32),
+        pltpu.VMEM(block, F32),
         pltpu.VMEM((slabs,) + block, F32),
         pltpu.VMEM((2, slabs) + block, F32),
         pltpu.VMEM((slabs,) + block, F32),

time: 143 us -> 96.1 us (0.67)
  the two profiles are of different devices: /device:TPU:193 before, /device:TPU:224 now
where the time goes in v2:
time: 96.1 us; the launch traced here: 94.8 us
  Pallas kernels  89.7 us (93%)
  local copies, waits for them, and re-layouts  4.42 us (5%)
    pallas_call x1, Pallas kernels, per_device(): pl.pallas_call(functools.partial(kernel, ne, nz), out_shape=(jax.ShapeDty...  89.7 us
    unnamed x2, local copies, waits for them, and re-layouts  4.42 us

profile of v2, /device:TPU:224, one launch (start us, length us, event | category | flops | bytes accessed | tf_op | source)
XLA Modules:
  0.0 94.8 jit_solution(7361627815754949630)
XLA Ops:
  0.6 89.7 %shard_map.104 = (f32[16,4,128]{2,1,0:T(4,128)}, f32[1,4,2,256,256]{4,3,2,1,0:T(8,128)}) custom-call(f32[16,4,128]{2,1,0:T(4,128)} %pot.1, f32[16,4,128]{2,1,0:T(4,128)} %charge.1, f32[16,4,128]{2,1,0:T(4,128)} %perm.1, s32[4,256]{1,0:T(4,128)} %owner.1, f32[1,4,2,256,256]{4,3,2,1,0:T(8,128)} %g_hbm.1, f32[4,2,256,256]{3,2,1,0:T(8,128)} %cpl_hbm.1, ...), custom_call_target="tpu_custom_call" | custom-call | tf_op jit(solution)/shard_map/pallas_call | solution.py:657
  90.3 1.4 %copy.13 = f32[16,4,128]{2,1,0:T(4,128)} copy(f32[16,4,128]{2,1,0:T(4,128)} %get-tuple-element.4) | data formatting | bytes 65536
  91.7 3.0 %copy.14 = f32[1,4,2,256,256]{4,3,2,1,0:T(8,128)} copy(f32[1,4,2,256,256]{4,3,2,1,0:T(8,128)} %get-tuple-element.5) | data formatting | bytes 4194304

commit v3 on v2

--- a/solution.py
+++ b/solution.py
@@ -12,6 +12,7 @@
 BF16 = jnp.bfloat16
 MESH = pl.DeviceIdType.MESH
 K_PIECES = 8
+K_AHEAD = 2
 
 
 def split(x):
@@ -35,17 +36,21 @@
 def kernel(
     ne,
     nz,
-    pot,
-    charge,
-    perm,
-    owner,
+    pot_hbm,
+    charge_hbm,
+    perm_hbm,
+    owner_hbm,
     g_hbm,
     cpl_hbm,
     shifts,
     occ,
     tiles_hbm,
     pot_out,
-    se_hbm,
+    se_out,
+    pot,
+    charge,
+    perm,
+    owner,
     g,
     cpl,
     tiles,
@@ -80,13 +85,12 @@
     state_in,
     k_in,
     k_out,
-    carry,
+    base,
     greens,
     greens_nb,
     sib_own,
     sib_nb,
     weight,
-    se,
     send_sem,
     recv_sem,
     local_sem,
@@ -122,7 +126,9 @@
             device_id_type=MESH,
         )
 
-    HALO, ROW, COL, GEX = 0, 4, 11, 14
+    HALO, ROW = 0, 4
+    COL = ROW + row - 1
+    GEX = COL + cols - 1
     PAIR = GEX + 2 * slabs
     KUP, KDOWN, KBACK = (PAIR + 2 + i * K_PIECES for i in range(3))
     KSIDE = KUP
@@ -131,19 +137,28 @@
     SIB = CARRY + 2
     SIBN = SIB + slabs
 
+    load_small = [
+        pltpu.make_async_copy(source, target, local_sem.at[3 + i])
+        for i, (source, target) in enumerate(
+            ((pot_hbm, pot), (perm_hbm, perm), (charge_hbm, charge), (owner_hbm, owner))
+        )
+    ]
+    for copy in load_small:
+        copy.start()
     load_g = pltpu.make_async_copy(g_hbm.at[0], g, local_sem.at[0])
     load_c = pltpu.make_async_copy(cpl_hbm, cpl, local_sem.at[1])
     load_t = pltpu.make_async_copy(tiles_hbm, tiles, local_sem.at[2])
-    load_g.start()
-    load_c.start()
-    load_t.start()
-
     partners = [in_row(k) for k in range(1, row)] + [energy(row * k) for k in range(1, cols)]
     partners += [energy(by) for by in (1, -1, 2, -2)] + [level(by) for by in (1, -1, 2, -2)]
     barrier = pltpu.get_barrier_semaphore()
     for device in partners:
         pl.semaphore_signal(barrier, inc=1, device_id=device, device_id_type=MESH)
 
+    load_g.start()
+    load_c.start()
+    load_t.start()
+    load_small[0].wait()
+    load_small[1].wait()
     for index, ref in enumerate((pot, perm)):
         hs_lo[index] = ref[:, 0:1, :]
         hs_hi[index] = ref[:, n1 - 1 : n1, :]
@@ -169,7 +184,7 @@
         )
 
     load_c.wait()
-    EVEN, ODD, BOTH, HALF = range(4)
+    EVEN, ODD, BOTH, HALF, FIRST = range(5)
 
     def keep(high, low, at, parts):
         for k, (h, l) in enumerate(split3(*parts)):
@@ -235,6 +250,8 @@
         windows.append(
             tuple(jnp.where(lane == edge, 0.0, pltpu.roll(x, shift, 2)) for x in (field, centre))
         )
+    load_small[2].wait()
+    load_small[3].wait()
     numerator = charge[...]
     denominator = jnp.zeros_like(numerator)
     for near_field, near_perm in windows:
@@ -309,10 +326,10 @@
         make_sources(s, (2, g, (s,)))
 
     sandwiches(
-        (lambda: link(2, 1), lambda: three(src, 2, 0), added(carry, (), (src, (2, 1)))),
+        (lambda: link(2, 1), lambda: three(src, 2, 0), added(base, (), (src, (2, 1)))),
         (lambda: link(2, 3), lambda: three(src, 2, 2), added(k_out, (), (src, (2, 3)))),
     )
-    sandwiches((lambda: mapping(HALF), lambda: three(carry), added(s_own, (), (k_out, ()))))
+    sandwiches((lambda: mapping(HALF), lambda: three(base), added(s_own, (), (k_out, ()))))
 
     send_s = remote(s_own, s_even, PAIR + 1, level(1))
 
@@ -337,14 +354,32 @@
                 weight[2] = jnp.where(core == 0, raise_now, lower_now)
                 weight[3] = jnp.where(core == 0, lower_now, raise_now)
 
-    def prepare_neighbours():
-        @pl.loop(1, slabs)
-        def _(s):
+    def prepare_neighbours(first, last):
+        def one(s, nothing):
             for side in range(2):
                 g_copy(s, side == 0).wait_recv()
             both = [(side, g_nb, (side, s)) for side in range(2)]
             make_links(s, *both)
             make_sources(s, *both)
+
+            @pl.when(s > 1)
+            def _():
+                sandwiches(
+                    *(
+                        (
+                            lambda side=side: link(side, s),
+                            lambda side=side: three(src, side, s - 1),
+                            added(src, (side, s), (src, (side, s))),
+                        )
+                        for side in range(2)
+                    )
+                )
+                for side in range(2):
+                    keep(link_h, link_l, (side, s), cprod(link(side, s), link(side, s - 1)))
+
+            return nothing
+
+        lax.fori_loop(first, last, one, 0)
 
     make_weights()
 
@@ -364,8 +399,9 @@
     k_up = [k_piece(k_out, KUP, i, level(2)) for i in pieces]
     k_down = [k_piece(k_in, KDOWN, i, level(-1)) for i in pieces]
     k_side = [k_piece(k_in, KSIDE, i, level(1)) for i in pieces]
-    k_back = [k_piece(k_out, KBACK, i, level(-2)) for i in pieces]
-    k_relay = [k_piece(k_in, KBACK, i, level(-2)) for i in pieces]
+    through_ring = range(K_AHEAD, K_PIECES)
+    k_back = {i: k_piece(k_out, KBACK, i, level(-2)) for i in through_ring}
+    k_relay = {i: k_piece(k_in, KBACK, i, level(-2)) for i in through_ring}
     ahead = [
         remote(p_even, map_in, AHEAD, level(1)),
         remote(s_own, state_in, AHEAD + 1, level(1)),
@@ -384,20 +420,31 @@
         send_p.wait_recv()
         keep(map_h, map_l, (EVEN,), (p_even[0], p_even[1]))
 
-    def into_carry(which, state):
-        sandwiches((lambda: mapping(which), lambda: three(k_in), added(carry, (), (state, ()))))
-
-    def receive_and_hand_on(copies, *onward):
-        for i in pieces:
+    def own_green(s, outer, ref, at, term):
+        sandwiches((outer, lambda: three(ref, *at), added(greens, (s,), term)))
+
+    def map_through(which):
+        keep(map_h, map_l, (FIRST,), cprod(link(2, 0), mapping(which)))
+
+    def add_through(state):
+        sandwiches(
+            (lambda: link(2, 0), lambda: three(state), added(base, (), (src, (2, 0))))
+        )
+
+    def first_green():
+        own_green(0, lambda: mapping(FIRST), k_in, (), (base, ()))
+
+    def receive_and_hand_on(copies, *onward, these=pieces):
+        for i in these:
             copies[i].wait_recv()
             for copy in onward:
                 copy[i].start()
 
-    early = jnp.logical_or(jnp.logical_not(odd), z > 4)
+    early = jnp.where(z >= 6, slabs - 1, jnp.where(odd, 1, slabs))
 
     @pl.when(z == 0)
     def _():
-        carry[...] = jnp.zeros_like(carry)
+        greens[0] = src[2, 0]
 
     @pl.when(z == 1)
     def _():
@@ -405,7 +452,7 @@
         k_out[...] = s_own[...]
         for copy in k_up:
             copy.start()
-        carry[...] = s_even[...]
+        own_green(0, lambda: link(2, 0), s_even, (), (src, (2, 0)))
 
     @pl.when(jnp.logical_or(z == 3, z == 5))
     def _():
@@ -428,12 +475,16 @@
         def _():
             ahead[1].start()
 
+        map_through(EVEN)
+        add_through(s_even)
+
     @pl.when(z == 7)
     def _():
         pair_maps()
         send_s.wait_recv()
         ahead[0].wait_recv()
         keep(map_h, map_l, (BOTH,), cprod(mapping(EVEN), three(map_in)))
+        map_through(BOTH)
 
     @pl.when(z == 6)
     def _():
@@ -441,18 +492,19 @@
             copy.wait_recv()
             relay.start()
         keep(map_h, map_l, (BOTH,), (map_in[0], map_in[1]))
-
-    @pl.when(early)
-    def _():
-        prepare_neighbours()
+        map_through(BOTH)
+        add_through(state_in)
+
+    prepare_neighbours(1, early)
 
     @pl.when(z == 3)
     def _():
         receive_and_hand_on(k_up, k_down)
         sandwiches((lambda: mapping(BOTH), lambda: three(k_in), added(k_out, (), (s_own, ()))))
-        for forward, backward in zip(k_up, k_back):
-            backward.start()
-            forward.start()
+        for i in pieces:
+            k_up[i].start()
+        for i in through_ring:
+            k_back[i].start()
 
     @pl.when(z == 5)
     def _():
@@ -460,7 +512,7 @@
 
     @pl.when(jnp.logical_or(z == 3, z == 5))
     def _():
-        into_carry(EVEN, s_even)
+        first_green()
 
     @pl.when(z == 7)
     def _():
@@ -468,18 +520,21 @@
         sandwiches(
             (lambda: mapping(EVEN), lambda: three(state_in), added(k_out, (), (s_even, ())))
         )
-        receive_and_hand_on(k_back)
-        into_carry(BOTH, k_out)
+        add_through(k_out)
+        receive_and_hand_on(k_side, these=range(K_AHEAD))
+        receive_and_hand_on(k_back, these=through_ring)
+        first_green()
 
     @pl.when(jnp.logical_or(z == 2, z == 4))
     def _():
         receive_and_hand_on(k_down)
-        carry[...] = k_in[...]
+        own_green(0, lambda: link(2, 0), k_in, (), (src, (2, 0)))
 
     @pl.when(z == 6)
     def _():
-        receive_and_hand_on(k_side)
-        into_carry(BOTH, state_in)
+        receive_and_hand_on(k_side, k_side, these=range(K_AHEAD))
+        receive_and_hand_on(k_side, these=through_ring)
+        first_green()
 
     def first_copy(side):
         return remote(
@@ -492,76 +547,69 @@
     def own_copy(s):
         return remote(greens.at[s], sib_own.at[s], SIB + s, sibling)
 
-    def own_green(s, ref, at):
-        sandwiches(
-            (lambda: link(2, s), lambda: three(ref, *at), added(greens, (s,), (src, (2, s))))
-        )
-
-    own_green(0, carry, ())
     for side in range(2):
         first_copy(side).start()
     own_copy(0).start()
 
     @pl.loop(1, slabs)
     def _(s):
-        own_green(s, greens, (s - 1,))
+        own_green(s, lambda: link(2, s), greens, (s - 1,), (src, (2, s)))
         own_copy(s).start()
 
     @pl.when(z == 1)
     def _():
-        receive_and_hand_on(k_back, k_relay)
-
-    @pl.when(jnp.logical_not(early))
-    def _():
-        prepare_neighbours()
+        receive_and_hand_on(k_back, k_relay, these=through_ring)
+
+    prepare_neighbours(early, slabs)
 
     def far_copy(side, s):
         return remote(greens_nb.at[side, s], sib_nb.at[s], SIBN + s, sibling)
 
-    def far_green(side, s):
+    def far_greens(side, use):
+        def write(s):
+            return lambda *made: use(s, *(made[part] + src[side, s, part] for part in range(2)))
+
         sandwiches(
-            (
-                lambda: link(side, s),
-                lambda: three(greens_nb, side, s - 1),
-                added(greens_nb, (side, s), (src, (side, s))),
+            *(
+                (lambda s=s: link(side, s), lambda: three(greens_nb, side, 0), write(s))
+                for s in range(1, slabs)
             )
         )
 
-    def se_copy(s):
-        return pltpu.make_async_copy(se.at[s], se_hbm.at[0, s], local_sem.at[3 + s])
-
-    def mix(s):
-        own_copy(s).wait_recv()
-        far_copy(0, s).wait_recv()
-        for part in range(2):
-            se[s, part] = (
-                weight[0] * greens_nb[0, s, part]
-                + weight[1] * greens_nb[1, s, part]
-                + weight[2] * sib_own[s, part]
-                + weight[3] * sib_nb[s, part]
-            )
-        se_copy(s).start()
+    def mix_most(s, part, near):
+        se_out[0, s, part] = (
+            weight[core] * near
+            + weight[1 - core] * greens_nb[1 - core, s, part]
+            + weight[2] * sib_own[s, part]
+        )
 
     for side in range(2):
         first_copy(side).wait_recv()
     far_copy(1 - core, 0).start()
 
-    @pl.loop(1, slabs)
+    def store_and_send(s, real, imag):
+        greens_nb[1 - core, s, 0], greens_nb[1 - core, s, 1] = real, imag
+        far_copy(1 - core, s).start()
+
+    def mix_both(s, real, imag):
+        mix_most(s, 0, real)
+        mix_most(s, 1, imag)
+
+    far_greens(1 - core, store_and_send)
+    for s in range(slabs):
+        own_copy(s).wait_recv()
+    mix_both(0, greens_nb[core, 0, 0], greens_nb[core, 0, 1])
+    far_greens(core, mix_both)
+
+    @pl.loop(0, slabs)
     def _(s):
-        far_green(1 - core, s)
-        far_copy(1 - core, s).start()
-
-    @pl.loop(1, slabs)
-    def _(s):
-        far_green(core, s)
-        mix(s - 1)
-
-    mix(slabs - 1)
+        far_copy(0, s).wait_recv()
+        for part in range(2):
+            se_out[0, s, part] = se_out[0, s, part] + weight[3] * sib_nb[s, part]
 
     for s in range(slabs):
         own_copy(s).wait_send()
         far_copy(0, s).wait_send()
-        se_copy(s).wait()
     for s in range(1, slabs):
         g_copy(s, True).wait_send()
         g_copy(s, False).wait_send()
@@ -579,8 +627,9 @@
     sent(jnp.logical_or(z == 1, z == 3), *k_up)
     sent(jnp.logical_or(z == 3, z == 5), *k_down)
     sent(z == 5, *k_side)
-    sent(z == 3, *k_back)
-    sent(z == 1, *k_relay)
+    sent(z == 6, *k_side[:K_AHEAD])
+    sent(z == 3, *k_back.values())
+    sent(z == 1, *k_relay.values())
     sent(z == 5, *ahead)
     sent(z == 6, *ahead_relay)
 
@@ -607,8 +656,12 @@
     row = min(8, ne)
     cols = ne // row
     block = (2, n, n)
-    sems = 14 + 2 * slabs + 2 + 3 * K_PIECES + 2 + 2 + 2 * slabs
+    sems = 4 + row - 1 + cols - 1 + 2 * slabs + 2 + 3 * K_PIECES + 2 + 2 + 2 * slabs
     scratch = [
+        pltpu.VMEM((n0, n1, n2), F32),
+        pltpu.VMEM((n0, n1, n2), F32),
+        pltpu.VMEM((n0, n1, n2), F32),
+        pltpu.VMEM((slabs, n), jnp.int32),
         pltpu.VMEM((slabs,) + block, F32),
         pltpu.VMEM((slabs,) + block, F32),
         pltpu.VMEM((modes, n, n), F32),
@@ -636,9 +689,9 @@
         pltpu.VMEM(block, F32),
         pltpu.VMEM(block, F32),
         pltpu.VMEM(block, F32),
-        pltpu.VMEM((4, 3, n, n), BF16),
-        pltpu.VMEM((4, 3, n, n), BF16),
-        pltpu.VMEM((2,) + block, F32),
+        pltpu.VMEM((5, 3, n, n), BF16),
+        pltpu.VMEM((5, 3, n, n), BF16),
+        pltpu.VMEM((3,) + block, F32),
         pltpu.VMEM(block, F32),
         pltpu.VMEM(block, F32),
         pltpu.VMEM(block, F32),
@@ -649,22 +702,21 @@
         pltpu.VMEM((slabs,) + block, F32),
         pltpu.VMEM((slabs,) + block, F32),
         pltpu.VMEM((4, n, n), F32),
-        pltpu.VMEM((slabs,) + block, F32),
         pltpu.SemaphoreType.DMA((sems,)),
         pltpu.SemaphoreType.DMA((sems,)),
-        pltpu.SemaphoreType.DMA((3 + slabs,)),
+        pltpu.SemaphoreType.DMA((7,)),
     ]
     return pl.pallas_call(
         functools.partial(kernel, ne, nz),
         out_shape=(
-            jax.ShapeDtypeStruct((n0, n1, n2), F32),
-            jax.ShapeDtypeStruct((1, slabs) + block, F32),
+            pltpu.VMEM((n0, n1, n2), F32),
+            pltpu.VMEM((1, slabs) + block, F32),
         ),
-        in_specs=[vmem, vmem, vmem, vmem, hbm, hbm, smem, smem, hbm],
-        out_specs=(vmem, hbm),
+        in_specs=[hbm, hbm, hbm, hbm, hbm, hbm, smem, smem, hbm],
+        out_specs=(vmem, vmem),
         scratch_shapes=scratch,
         compiler_params=pltpu.CompilerParams(
-            collective_id=0, has_side_effects=True, vmem_limit_bytes=60 << 20
+            collective_id=0, has_side_effects=True, vmem_limit_bytes=54 << 20
         ),
     )(
         potential_old,

time: 96.1 us -> 90.3 us (0.940); the launches traced: 94.8 us -> 90.2 us
  local copies, waits for them, and re-layouts: 4.42 us -> 1.94 us
  Pallas kernels: 89.7 us -> 87.7 us
    unnamed x2, local copies, waits for them, and re-layouts: 4.42 us -> 1.94 us
    pallas_call x1, Pallas kernels: 89.7 us -> 87.7 us  [per_device(): pl.pallas_call(functools.partial(kernel, ne, nz), out_shape=(pltpu.VMEM((...]
where the time goes in v3:
time: 90.3 us; the launch traced here: 90.2 us
  Pallas kernels  87.7 us (97%)
  local copies, waits for them, and re-layouts  1.94 us (2%)
    pallas_call x1, Pallas kernels, per_device(): pl.pallas_call(functools.partial(kernel, ne, nz), out_shape=(pltpu.VMEM((...  87.7 us
    unnamed x2, local copies, waits for them, and re-layouts  1.94 us

profile of v3, /device:TPU:224, one launch (start us, length us, event | category | flops | bytes accessed | tf_op | source)
XLA Modules:
  0.0 90.2 jit_solution(8450337892831417487)
XLA Ops:
  0.6 87.7 %shard_map.104 = (f32[16,4,128]{2,1,0:T(4,128)S(1)}, f32[1,4,2,256,256]{4,3,2,1,0:T(8,128)S(1)}) custom-call(f32[16,4,128]{2,1,0:T(4,128)} %pot_hbm.1, f32[16,4,128]{2,1,0:T(4,128)} %charge_hbm.1, f32[16,4,128]{2,1,0:T(4,128)} %perm_hbm.1, s32[4,256]{1,0:T(4,128)} %owner_hbm.1, f32[1,4,2,256,256]{4,3,2,1,0:T(8,128)} %g_hbm.1, f32[4,2,256,256]{3,2,1,0:T(8,128)} %cpl_hbm.1, ...), custom_call_target="tpu_custom_call" | custom-call | tf_op jit(solution)/shard_map/pallas_call | solution.py:709
  88.3 0.6 copy.13
  88.9 1.3 %copy.14 = f32[1,4,2,256,256]{4,3,2,1,0:T(8,128)} copy(f32[1,4,2,256,256]{4,3,2,1,0:T(8,128)S(1)} %get-tuple-element.3) | data formatting | bytes 4194304

commit v4 on v3

--- a/solution.py
+++ b/solution.py
@@ -12,7 +12,7 @@
 BF16 = jnp.bfloat16
 MESH = pl.DeviceIdType.MESH
 K_PIECES = 8
-K_AHEAD = 2
+K_AHEAD = 1
 
 
 def split(x):
@@ -501,10 +501,10 @@
     def _():
         receive_and_hand_on(k_up, k_down)
         sandwiches((lambda: mapping(BOTH), lambda: three(k_in), added(k_out, (), (s_own, ()))))
+        for i in through_ring:
+            k_back[i].start()
         for i in pieces:
             k_up[i].start()
-        for i in through_ring:
-            k_back[i].start()
 
     @pl.when(z == 5)
     def _():

time: 90.3 us -> 89.3 us (0.989)
  Pallas kernels: 87.7 us -> 86.6 us
    pallas_call x1, Pallas kernels: 87.7 us -> 86.6 us  [per_device(): pl.pallas_call(functools.partial(kernel, ne, nz), out_shape=(pltpu.VMEM((...]
where the time goes in v4:
time: 89.3 us; the launch traced here: 89.2 us
  Pallas kernels  86.6 us (97%)
  local copies, waits for them, and re-layouts  1.94 us (2%)
    pallas_call x1, Pallas kernels, per_device(): pl.pallas_call(functools.partial(kernel, ne, nz), out_shape=(pltpu.VMEM((...  86.6 us
    unnamed x2, local copies, waits for them, and re-layouts  1.94 us

profile of v4, /device:TPU:224, one launch (start us, length us, event | category | flops | bytes accessed | tf_op | source)
XLA Modules:
  0.0 89.2 jit_solution(16077708777148139284)
XLA Ops:
  0.6 86.6 %shard_map.104 = (f32[16,4,128]{2,1,0:T(4,128)S(1)}, f32[1,4,2,256,256]{4,3,2,1,0:T(8,128)S(1)}) custom-call(f32[16,4,128]{2,1,0:T(4,128)} %pot_hbm.1, f32[16,4,128]{2,1,0:T(4,128)} %charge_hbm.1, f32[16,4,128]{2,1,0:T(4,128)} %perm_hbm.1, s32[4,256]{1,0:T(4,128)} %owner_hbm.1, f32[1,4,2,256,256]{4,3,2,1,0:T(8,128)} %g_hbm.1, f32[4,2,256,256]{3,2,1,0:T(8,128)} %cpl_hbm.1, ...), custom_call_target="tpu_custom_call" | custom-call | tf_op jit(solution)/shard_map/pallas_call | solution.py:709
  87.3 0.6 copy.13
  87.9 1.3 %copy.14 = f32[1,4,2,256,256]{4,3,2,1,0:T(8,128)} copy(f32[1,4,2,256,256]{4,3,2,1,0:T(8,128)S(1)} %get-tuple-element.3) | data formatting | bytes 4194304

commit v5 on v4

--- a/solution.py
+++ b/solution.py
@@ -11,8 +11,8 @@
 F32 = jnp.float32
 BF16 = jnp.bfloat16
 MESH = pl.DeviceIdType.MESH
-K_PIECES = 8
-K_AHEAD = 1
+K_PIECES = 16
+K_AHEAD = 2
 
 
 def split(x):

time: 89.3 us -> 89.8 us (level)
  no operation moved by 1% of the time
where the time goes in v5:
time: 89.8 us; the launch traced here: 89.7 us
  Pallas kernels  87.1 us (97%)
  local copies, waits for them, and re-layouts  1.94 us (2%)
    pallas_call x1, Pallas kernels, per_device(): pl.pallas_call(functools.partial(kernel, ne, nz), out_shape=(pltpu.VMEM((...  87.1 us
    unnamed x2, local copies, waits for them, and re-layouts  1.94 us

profile of v5, /device:TPU:224, one launch (start us, length us, event | category | flops | bytes accessed | tf_op | source)
XLA Modules:
  0.0 89.7 jit_solution(4761461382095298275)
XLA Ops:
  0.6 87.1 %shard_map.104 = (f32[16,4,128]{2,1,0:T(4,128)S(1)}, f32[1,4,2,256,256]{4,3,2,1,0:T(8,128)S(1)}) custom-call(f32[16,4,128]{2,1,0:T(4,128)} %pot_hbm.1, f32[16,4,128]{2,1,0:T(4,128)} %charge_hbm.1, f32[16,4,128]{2,1,0:T(4,128)} %perm_hbm.1, s32[4,256]{1,0:T(4,128)} %owner_hbm.1, f32[1,4,2,256,256]{4,3,2,1,0:T(8,128)} %g_hbm.1, f32[4,2,256,256]{3,2,1,0:T(8,128)} %cpl_hbm.1, ...), custom_call_target="tpu_custom_call" | custom-call | tf_op jit(solution)/shard_map/pallas_call | solution.py:709
  87.8 0.6 copy.13
  88.4 1.3 %copy.14 = f32[1,4,2,256,256]{4,3,2,1,0:T(8,128)} copy(f32[1,4,2,256,256]{4,3,2,1,0:T(8,128)S(1)} %get-tuple-element.3) | data formatting | bytes 4194304
